TPU v7x, 32 devices: a whole 2x2x4 slice. The times are simulated.
32 devices in a mesh: groups: 2 (over x), pool: 2 (over core), tensor: 8 (over z, y).
Axes of the slice: x: 2, y: 2, z: 4, core: 2. Of those that a mesh axis runs over, the one named last changes fastest.
Arguments:
- hidden: bfloat16 [64, 5120], P(('groups', 'pool', 'tensor')), parts along dimension 0, may hold values from -1.5 to 1.5
- input_gain: float32 [5120], replicated, may hold values from 0.1 to 1.9
- query_weight: bfloat16 [5120, 4096], P(None, ('pool', 'tensor')), may hold values from -0.078125 to 0.078125
- key_weight: bfloat16 [5120, 512], P(None, ('pool', 'tensor')), may hold values from -0.078125 to 0.078125
- value_weight: bfloat16 [5120, 512], P(None, ('pool', 'tensor')), may hold values from -0.078125 to 0.078125
- query_gain: float32 [128], replicated, may hold values from 2 to 6
- key_gain: float32 [128], replicated, may hold values from 1 to 4
- output_weight: bfloat16 [4096, 5120], P(('pool', 'tensor')), may hold values from -0.09375 to 0.09375
- post_gain: float32 [5120], replicated, may hold values from 0.1 to 1.9
- gate_weight: bfloat16 [5120, 12800], P(None, ('pool', 'tensor')), may hold values from -0.078125 to 0.078125
- up_weight: bfloat16 [5120, 12800], P(None, ('pool', 'tensor')), may hold values from -0.078125 to 0.078125
- down_weight: bfloat16 [12800, 5120], P(('pool', 'tensor')), may hold values from -0.0546875 to 0.0546875
- key_cache: bfloat16 [65536, 512], P(('groups', 'pool', 'tensor')), parts along dimension 0, may hold values from -45 to 45
- value_cache: bfloat16 [65536, 512], P(('groups', 'pool', 'tensor')), parts along dimension 0, may hold values from -6 to 6
- lengths: int32 [64], P('groups'), parts along dimension 0, may hold values from 128 to 2048, as said below
- request_slot: int32 [64], P('groups'), parts along dimension 0, may hold values from 0 to 63, as said below
Outputs:
- mixed: bfloat16 [64, 5120], P(('groups', 'pool', 'tensor')), parts along dimension 0
- final: bfloat16 [64, 5120], P(('groups', 'pool', 'tensor')), parts along dimension 0
There are 2 independent parts, one for each index of `groups`. A program takes and returns all parts, laid end to end along the dimension named above; an argument that names none is the same for every part. Nothing has to cross between parts.
Inputs may be any that keep to these rules, and one draw needn't show every extreme that they name: `request_slot`: each owner holds at most 4 requests and some owner holds exactly 4; no two requests share a slot. The lengths of one owner's requests sum to at most 2048; some request has exactly 2048 and some exactly 128.
All inputs are finite; a program needn't handle non-finite values.
Results may differ from a plain program's by a relative error of at most 0.03.
The roundings to bfloat16 on the way count: a program that leaves them out, or rounds other values in their place, can miss the bound.
Values may be sent and summed in bfloat16 or wider, within the bound.
A program may use at most 64 MiB of HBM per device.

v0:
```python
import functools
import math

import jax
import jax.numpy as jnp
import numpy as np
from jax import lax
from jax.experimental import pallas as pl
from jax.experimental.pallas import tpu as pltpu
from jax.sharding import PartitionSpec as P

SLOTS = 4


eps = 1e-06
theta = 1000000.0


def rms_scale(values, scales):
    values = values.astype(jnp.float32)
    return values * lax.rsqrt(jnp.mean(values * values, axis=-1, keepdims=True) + eps) * scales


def rotate(values, position):
    half_width = values.shape[-1] // 2
    frequency = theta ** (-jnp.arange(half_width, dtype=jnp.float32) * 2.0 / values.shape[-1])
    angles = position * frequency
    cosine = jnp.cos(angles)
    sine_part = jnp.sin(angles)
    front_half = values[..., :half_width]
    back_half = values[..., half_width:]
    return jnp.concatenate(
        [front_half * cosine - back_half * sine_part, back_half * cosine + front_half * sine_part],
        axis=-1,
    )


def on_device(
    hidden,
    input_gain,
    query_weight,
    key_weight,
    value_weight,
    query_gain,
    key_gain,
    output_weight,
    post_gain,
    gate_weight,
    up_weight,
    down_weight,
    key_cache,
    value_cache,
    lengths,
    request_slot,
):
    devices = lax.axis_size(("pool", "tensor"))
    device_index = lax.axis_index(("pool", "tensor"))
    local_rows = hidden.shape[0]
    query_cols = query_weight.shape[1]
    key_cols = key_weight.shape[1]
    width_sent = query_cols + 2 * key_cols
    head_dim = query_gain.shape[0]
    slot_count = SLOTS
    head_count = devices * query_cols // head_dim
    kv_count = devices * key_cols // head_dim
    group_size = head_count // kv_count
    normed = rms_scale(hidden, input_gain).astype(jnp.bfloat16)
    shard_rows = lax.all_gather(normed, ("pool", "tensor"), axis=0, tiled=True)
    query_part = jnp.dot(shard_rows, query_weight, preferred_element_type=jnp.float32)
    key_part = jnp.dot(shard_rows, key_weight, preferred_element_type=jnp.float32)
    value_part = jnp.dot(shard_rows, value_weight, preferred_element_type=jnp.float32)
    projected = jnp.concatenate([query_part, key_part, value_part], axis=1).astype(jnp.bfloat16)
    outgoing = (
        jnp.zeros((devices * slot_count, width_sent), jnp.bfloat16).at[request_slot].set(projected)
    )
    outgoing = outgoing.reshape(devices, slot_count, width_sent)
    arrived = lax.all_to_all(
        outgoing, ("pool", "tensor"), split_axis=0, concat_axis=2, tiled=True
    ).reshape(slot_count, devices, width_sent)
    query_full = arrived[:, :, :query_cols].reshape(slot_count, head_count, head_dim)
    key_full = arrived[:, :, query_cols : query_cols + key_cols].reshape(
        slot_count, kv_count, head_dim
    )
    value_new = arrived[:, :, query_cols + key_cols :].reshape(slot_count, kv_count, head_dim)
    slot_ids = device_index * slot_count + jnp.arange(slot_count, dtype=jnp.int32)
    matches = request_slot[None, :] == slot_ids[:, None]
    slot_length = jnp.sum(jnp.where(matches, lengths[None, :], 0), axis=1)
    owner_of = request_slot // slot_count
    within = request_slot % slot_count
    earlier = (owner_of[None, :] == device_index) & (
        within[None, :] < jnp.arange(slot_count, dtype=jnp.int32)[:, None]
    )
    slot_offset = jnp.sum(jnp.where(earlier, lengths[None, :], 0), axis=1)
    position = slot_length.astype(jnp.float32)[:, None, None]
    query_heads = rotate(rms_scale(query_full, query_gain), position).astype(jnp.bfloat16)
    query_heads = query_heads.reshape(slot_count, kv_count, group_size, head_dim)
    key_new = rotate(rms_scale(key_full, key_gain), position).astype(jnp.bfloat16)
    pool_tokens = key_cache.shape[0]
    cached_keys = key_cache.reshape(pool_tokens, kv_count, head_dim)
    cached_values = value_cache.reshape(pool_tokens, kv_count, head_dim)
    scale_factor = 1.0 / math.sqrt(head_dim)
    scores = (
        jnp.einsum("skgd,tkd->skgt", query_heads, cached_keys, preferred_element_type=jnp.float32)
        * scale_factor
    )
    own_score = (
        jnp.einsum("skgd,skd->skg", query_heads, key_new, preferred_element_type=jnp.float32)
        * scale_factor
    )
    token_pos = jnp.arange(pool_tokens, dtype=jnp.int32)
    inside = (token_pos[None, :] >= slot_offset[:, None]) & (
        token_pos[None, :] < (slot_offset + slot_length)[:, None]
    )
    inside = inside[:, None, None, :]
    largest = jnp.maximum(jnp.max(jnp.where(inside, scores, -1e30), axis=3), own_score)
    weights = jnp.where(inside, jnp.exp(scores - largest[..., None]), 0.0)
    own_weight = jnp.exp(own_score - largest)
    denominator = jnp.sum(weights, axis=3) + own_weight
    summed = jnp.einsum(
        "skgt,tkd->skgd",
        weights.astype(jnp.bfloat16),
        cached_values,
        preferred_element_type=jnp.float32,
    )
    own_low = own_weight.astype(jnp.bfloat16).astype(jnp.float32)
    summed = summed + own_low[..., None] * value_new.astype(jnp.float32)[:, :, None, :]
    head_out = (
        (summed / denominator[..., None])
        .astype(jnp.bfloat16)
        .reshape(slot_count, devices, query_cols)
    )
    returned = lax.all_to_all(head_out, ("pool", "tensor"), split_axis=1, concat_axis=0, tiled=True)
    head_rows = returned.reshape(devices * slot_count, query_cols)[request_slot]
    partial_value = jnp.dot(head_rows, output_weight, preferred_element_type=jnp.float32)
    row_start = device_index * local_rows
    own_part = lax.dynamic_slice_in_dim(partial_value, row_start, local_rows, 0) + hidden.astype(
        jnp.float32
    )
    partial_value = lax.dynamic_update_slice_in_dim(partial_value, own_part, row_start, 0)
    totals = lax.psum(partial_value, ("pool", "tensor"))
    mixed_all = totals.astype(jnp.bfloat16)
    mixed_rows = lax.dynamic_slice_in_dim(mixed_all, row_start, local_rows, 0)
    post_normed = rms_scale(mixed_all, post_gain).astype(jnp.bfloat16)
    gate_part = jnp.dot(post_normed, gate_weight, preferred_element_type=jnp.float32)
    up_part = jnp.dot(post_normed, up_weight, preferred_element_type=jnp.float32)
    activated = (jax.nn.silu(gate_part) * up_part).astype(jnp.bfloat16)
    lowered = lax.psum_scatter(
        jnp.dot(activated, down_weight, preferred_element_type=jnp.float32),
        ("pool", "tensor"),
        scatter_dimension=0,
        tiled=True,
    )
    final_rows = (mixed_rows.astype(jnp.float32) + lowered).astype(jnp.bfloat16)
    return (mixed_rows, final_rows)


MESH = pl.DeviceIdType.MESH
F32 = jnp.float32
SPLIT = 2
BF16 = jnp.bfloat16


def step_kernel(
    pool,
    tensor,
    hidden_ref,
    input_gain_ref,
    query_gain_ref,
    key_gain_ref,
    post_gain_ref,
    length_ref,
    slot_ref,
    frequency_ref,
    qw_hbm,
    kw_hbm,
    vw_hbm,
    ow_hbm,
    gw_hbm,
    uw_hbm,
    dw_hbm,
    kc_hbm,
    vc_hbm,
    mixed_ref,
    added_ref,
    qw,
    kw,
    vw,
    ow,
    gw,
    uw,
    dw,
    kc,
    vc,
    ag1,
    ag2,
    xs,
    slots,
    to_owner,
    at_owner,
    qs,
    kvs,
    ho,
    to_home,
    at_home,
    back,
    part1,
    peer1,
    out1,
    in1,
    part2,
    peer2,
    out2,
    in2,
    load_sem,
    ag1_s,
    ag1_r,
    ag2_s,
    ag2_r,
    a1_s,
    a1_r,
    a2_s,
    a2_r,
    rs1_s,
    rs1_r,
    rs2_s,
    rs2_r,
):
    devices = pool * tensor
    rows, width = hidden_ref.shape
    requests = devices * rows
    head_dim = query_gain_ref.shape[1]
    query_cols = qw.shape[1]
    key_cols = kw.shape[0]
    heads_here = query_cols // head_dim
    head_count = devices * heads_here
    kv_count = devices * key_cols // head_dim
    per_kv = devices // kv_count
    group = head_count // kv_count
    hidden_units = gw.shape[0]
    p = lax.axis_index("pool")
    t = lax.axis_index("tensor")
    me = p * tensor + t
    partner = {"pool": 1 - p, "tensor": t}

    loads = [
        pltpu.make_async_copy(a, b, load_sem.at[i])
        for i, (a, b) in enumerate(
            [
                (qw_hbm, qw),
                (kw_hbm, kw),
                (vw_hbm, vw),
                (kc_hbm, kc),
                (vc_hbm, vc),
                (ow_hbm, ow),
                (gw_hbm, gw),
                (uw_hbm, uw),
                (dw_hbm, dw),
            ]
        )
    ]
    for load in loads:
        load.start()

    def place(index):
        return {"pool": lax.div(index, tensor), "tensor": lax.rem(index, tensor)}

    def each(first, last, body):
        for j in range(first, last):
            body(j)

    barrier = pltpu.get_barrier_semaphore()
    each(
        1,
        devices,
        lambda j: pl.semaphore_signal(
            barrier, inc=1, device_id=place(lax.rem(me + j, devices)), device_id_type=MESH
        ),
    )

    def remote(source, target, sent, received, where):
        return pltpu.make_async_remote_copy(
            src_ref=source,
            dst_ref=target,
            send_sem=sent,
            recv_sem=received,
            device_id=where,
            device_id_type=MESH,
        )

    def gather(buffer, sent, received, lead, advance, carry):
        split = buffer.shape[0]

        def peer_copy(c, j):
            return remote(
                buffer.at[c, me],
                buffer.at[c, me],
                sent.at[c, j],
                received.at[c, me],
                {"pool": p, "tensor": lax.rem(t + j, tensor)},
            )

        def own_copy(c):
            return remote(
                buffer.at[c, me], buffer.at[c, me], sent.at[c, 0], received.at[c, me], partner
            )

        def passed(c, j):
            index = p * tensor + lax.rem(t + j, tensor)
            return remote(
                buffer.at[c, index],
                buffer.at[c, index],
                sent.at[c, tensor + j],
                received.at[c, index],
                partner,
            )

        def from_partner(c, j):
            index = (1 - p) * tensor + lax.rem(t + j, tensor)
            return remote(
                buffer.at[c, index],
                buffer.at[c, index],
                sent.at[c, 0],
                received.at[c, index],
                partner,
            )

        def forward(c, j):
            passed(c, j).wait_recv()
            passed(c, j).start()

        for c in range(split):
            each(1, tensor, lambda j: peer_copy(c, j).start())
            own_copy(c).start()
        each(1, tensor, lambda j: forward(0, j))
        steps = width // split // chunk
        for c in range(split):
            each(0, tensor, lambda j: from_partner(c, j).wait_recv())
            for index in range(devices):
                xs[index * rows : (index + 1) * rows, c * width // split : (c + 1) * width // split] = (
                    buffer[c, index].astype(F32)
                )
            first = c * steps
            if c + 1 < split:
                lead = min(lead, steps)
                carry = lax.fori_loop(first, first + lead, advance, carry)
                each(1, tensor, lambda j: forward(c + 1, j))
                first = first + lead
            carry = lax.fori_loop(first, (c + 1) * steps, advance, carry)

        def finish():
            for c in range(split):
                own_copy(c).wait_send()
                each(1, tensor, lambda j: peer_copy(c, j).wait_send())
                each(1, tensor, lambda j: passed(c, j).wait_send())

        return carry, finish

    def exchange(outgoing, incoming, sent, received):
        def copy(j):
            peer = lax.rem(me + j, devices)
            return remote(
                outgoing.at[peer], incoming.at[me], sent.at[j], received.at[me], place(peer)
            )

        def arrival(j):
            peer = lax.rem(me + j, devices)
            return remote(
                outgoing.at[peer], incoming.at[peer], sent.at[j], received.at[peer], place(peer)
            )

        each(1, devices, lambda j: copy(j).start())
        incoming[me] = outgoing[me]
        each(1, devices, lambda j: arrival(j).wait_recv())
        return lambda: each(1, devices, lambda j: copy(j).wait_send())

    def scatter_sum(left, weight, part, peer, outgoing, incoming, sent, received):
        split = part.shape[0]
        wide = width // split

        def swap(c):
            return remote(
                part.at[c, 1 - p], peer.at[c], sent.at[c, 0], received.at[c, tensor], partner
            )

        def copy(c, j):
            other = lax.rem(t + j, tensor)
            return remote(
                outgoing.at[c, other],
                incoming.at[c, t],
                sent.at[c, j],
                received.at[c, t],
                {"pool": p, "tensor": other},
            )

        def arrival(c, j):
            other = lax.rem(t + j, tensor)
            return remote(
                outgoing.at[c, other],
                incoming.at[c, other],
                sent.at[c, j],
                received.at[c, other],
                {"pool": p, "tensor": other},
            )

        for c in range(split):

            def columns(i, carry):
                near = pl.multiple_of(i * chunk, chunk)
                product = jnp.dot(
                    left, weight[:, pl.ds(c * wide + near, chunk)], preferred_element_type=F32
                )
                for q in range(pool):
                    part[c, q, :, pl.ds(near, chunk)] = product[
                        q * half : (q + 1) * half, :
                    ].astype(part.dtype)
                return carry

            lax.fori_loop(0, wide // chunk, columns, 0)
            swap(c).start()
        for c in range(split):
            swap(c).wait_recv()
            near = slice(c * wide, (c + 1) * wide)
            xs[:half, near] = peer[c].astype(F32) + part[c, p].astype(F32)
            for index in range(tensor):
                outgoing[c, index] = xs[index * rows : (index + 1) * rows, near].astype(BF16)
            each(1, tensor, lambda j: copy(c, j).start())
            incoming[c, t] = outgoing[c, t]
        totals = []
        for c in range(split):
            each(1, tensor, lambda j: arrival(c, j).wait_recv())
            total = incoming[c, 0].astype(F32)
            for index in range(1, tensor):
                total = total + incoming[c, index].astype(F32)
            totals.append(total)

        def finish():
            for c in range(split):
                swap(c).wait_send()
                each(1, tensor, lambda j: copy(c, j).wait_send())

        return jnp.concatenate(totals, axis=1), finish

    split = ag1.shape[0]
    chunk = math.gcd(width // split, 2560)
    half = tensor * rows

    def offer(buffer, values):
        wide = width // split
        for c in range(split):
            buffer[c, me] = values[:, c * wide : (c + 1) * wide].astype(BF16)

    hidden = hidden_ref[...].astype(F32)
    offer(ag1, rms_scale(hidden, input_gain_ref[...]))

    slot_row = slot_ref[...]
    length_row = length_ref[...]
    wide = devices * SLOTS
    scatter_hot = (
        lax.broadcasted_iota(jnp.int32, (wide, requests), 0) == slot_row
    ).astype(F32).astype(BF16)
    eye = lax.broadcasted_iota(jnp.int32, (requests, requests), 0) == lax.broadcasted_iota(
        jnp.int32, (requests, requests), 1
    )
    slot_col = jnp.sum(
        jnp.where(eye, jnp.broadcast_to(slot_row, (requests, requests)), 0).astype(F32),
        axis=1,
        keepdims=True,
    ).astype(jnp.int32)
    gather_hot = (
        lax.broadcasted_iota(jnp.int32, (requests, wide), 1) == slot_col
    ).astype(F32).astype(BF16)
    span = 2 * SLOTS
    place_id = lax.rem(lax.broadcasted_iota(jnp.int32, (span, requests), 0), SLOTS)
    slot_wide = jnp.broadcast_to(slot_row, (span, requests))
    length_wide = jnp.broadcast_to(length_row, (span, requests)).astype(F32)
    base = me * SLOTS
    slot_length = jnp.sum(
        jnp.where(slot_wide == base + place_id, length_wide, 0.0), axis=1, keepdims=True
    )
    slot_offset = jnp.sum(
        jnp.where((slot_wide >= base) & (slot_wide < base + place_id), length_wide, 0.0),
        axis=1,
        keepdims=True,
    )
    angles = slot_length * frequency_ref[...]
    cosine = jnp.cos(angles)
    lane = lax.broadcasted_iota(jnp.int32, (span, head_dim), 1)
    sine_part = jnp.where(lane < head_dim // 2, -jnp.sin(angles), jnp.sin(angles))
    pool_tokens = kc.shape[0]
    token = lax.broadcasted_iota(jnp.int32, (span, pool_tokens), 1).astype(F32)
    inside = jnp.where(
        (token >= slot_offset) & (token < slot_offset + slot_length), 1.0, 0.0
    )

    def turn(values, scale, copies):
        scaled = rms_scale(values, scale)
        return scaled * jnp.tile(cosine, (copies, 1)) + pltpu.roll(
            scaled, head_dim // 2, 1
        ) * jnp.tile(sine_part, (copies, 1))

    pl.semaphore_wait(barrier, devices - 1)
    for load in loads[:3]:
        load.wait()

    def turned(left, weight, at):
        return lax.dot_general(
            left, weight[:, at], (((1,), (1,)), ((), ())), preferred_element_type=F32
        )

    def project(i, carry):
        at = pl.ds(pl.multiple_of(i * chunk, chunk), chunk)
        left = xs[:, at].astype(BF16)
        return tuple(
            acc + product
            for acc, product in zip(
                carry,
                (
                    jnp.dot(left, qw[at, :], preferred_element_type=F32),
                    turned(left, kw, at),
                    turned(left, vw, at),
                ),
            )
        )

    (query_part, key_part, value_part), finish = gather(
        ag1,
        ag1_s,
        ag1_r,
        1,
        project,
        (
            jnp.zeros((requests, query_cols), F32),
            jnp.zeros((requests, key_cols), F32),
            jnp.zeros((requests, key_cols), F32),
        ),
    )

    done = [finish]

    def shift(count, amount):
        low = lax.broadcasted_iota(jnp.int32, (count, head_dim), 0)
        high = lax.broadcasted_iota(jnp.int32, (count, head_dim), 1)
        return (low + amount == high).astype(F32).astype(BF16)

    kv_part = jnp.dot(
        key_part.astype(BF16), shift(key_cols, 0), preferred_element_type=F32
    ) + jnp.dot(value_part.astype(BF16), shift(key_cols, key_cols), preferred_element_type=F32)
    slots[:, :query_cols] = jnp.dot(
        scatter_hot, query_part.astype(BF16), preferred_element_type=F32
    )
    slots[:, query_cols:] = jnp.dot(
        scatter_hot, kv_part.astype(BF16), preferred_element_type=F32
    )
    for index in range(devices):
        to_owner[index] = slots[index * SLOTS : (index + 1) * SLOTS, :].astype(BF16)
    done.append(exchange(to_owner, at_owner, a1_s, a1_r))

    for index in range(devices):
        arrived = at_owner[index].astype(F32)
        for j in range(heads_here):
            at = (index * heads_here + j) * SLOTS
            qs[at : at + SLOTS, :] = arrived[:, j * head_dim : (j + 1) * head_dim]
        at = (index // per_kv) * span
        lanes = (index % per_kv) * head_dim
        kvs[at : at + SLOTS, lanes : lanes + head_dim] = arrived[:, query_cols:]
        kvs[at + SLOTS : at + span, lanes : lanes + head_dim] = arrived[:, query_cols:]

    low = lax.broadcasted_iota(jnp.int32, (per_kv * head_dim, head_dim), 0)
    high = lax.broadcasted_iota(jnp.int32, (per_kv * head_dim, head_dim), 1)
    piece = lax.div(low, head_dim)
    inner = lax.rem(low, head_dim)
    key_hot = ((inner < key_cols) & (piece * key_cols + inner == high)).astype(F32).astype(BF16)
    value_hot = (
        ((inner >= key_cols) & (inner < 2 * key_cols) & (piece * key_cols + inner - key_cols == high))
        .astype(F32)
        .astype(BF16)
    )
    pieces = kvs[...].astype(BF16)
    key_new = turn(
        jnp.dot(pieces, key_hot, preferred_element_type=F32), key_gain_ref[...], kv_count
    ).astype(BF16)
    value_new = jnp.dot(pieces, value_hot, preferred_element_type=F32)
    scale_factor = 1.0 / math.sqrt(head_dim)
    block = group * SLOTS
    copies = block // span
    allowed = jnp.tile(inside, (copies, 1)) > 0.5
    for load in loads[3:5]:
        load.wait()
    for k in range(kv_count):
        query = turn(qs[k * block : (k + 1) * block, :], query_gain_ref[...], copies).astype(BF16)
        lanes = slice(k * head_dim, (k + 1) * head_dim)
        scores = (
            lax.dot_general(
                query, kc[:, lanes], (((1,), (1,)), ((), ())), preferred_element_type=F32
            )
            * scale_factor
        )
        own_key = jnp.tile(key_new[k * span : (k + 1) * span, :].astype(F32), (copies, 1))
        own_value = jnp.tile(value_new[k * span : (k + 1) * span, :], (copies, 1))
        own_score = jnp.sum(query.astype(F32) * own_key, axis=1, keepdims=True) * scale_factor
        scores = jnp.where(allowed, scores, -1e30)
        largest = jnp.maximum(jnp.max(scores, axis=1, keepdims=True), own_score)
        weights = jnp.exp(scores - largest)
        own_weight = jnp.exp(own_score - largest)
        denominator = jnp.sum(weights, axis=1, keepdims=True) + own_weight
        summed = jnp.dot(weights.astype(BF16), vc[:, lanes], preferred_element_type=F32)
        summed = summed + own_weight.astype(BF16).astype(F32) * own_value
        ho[k * block : (k + 1) * block, :] = summed / denominator
    for index in range(devices):
        for j in range(heads_here):
            at = (index * heads_here + j) * SLOTS
            to_home[index, :, j * head_dim : (j + 1) * head_dim] = ho[at : at + SLOTS, :].astype(BF16)
    done.append(exchange(to_home, at_home, a2_s, a2_r))
    for index in range(devices):
        back[index * SLOTS : (index + 1) * SLOTS, :] = at_home[index].astype(F32)
    head_rows = jnp.dot(
        gather_hot, back[...].astype(BF16), preferred_element_type=F32
    ).astype(BF16)

    loads[5].wait()
    total, finish = scatter_sum(head_rows, ow, part1, peer1, out1, in1, rs1_s, rs1_r)
    done.append(finish)
    mixed = (total + hidden).astype(BF16)
    mixed_ref[...] = mixed.astype(F32)
    offer(ag2, rms_scale(mixed, post_gain_ref[...]))
    loads[6].wait()
    loads[7].wait()

    def expand(i, carry):
        at = pl.ds(pl.multiple_of(i * chunk, chunk), chunk)
        left = xs[:, at].astype(BF16)
        return tuple(
            acc + turned(left, w, at)
            for acc, w in zip(carry, (gw, uw))
        )

    (gate_part, up_part), finish = gather(
        ag2,
        ag2_s,
        ag2_r,
        2,
        expand,
        (jnp.zeros((requests, hidden_units), F32), jnp.zeros((requests, hidden_units), F32)),
    )
    done.append(finish)
    activated = (gate_part / (1.0 + jnp.exp(-gate_part)) * up_part).astype(BF16)
    loads[8].wait()
    total, finish = scatter_sum(activated, dw, part2, peer2, out2, in2, rs2_s, rs2_r)
    done.append(finish)
    added_ref[...] = total
    for finish in done:
        finish()


def fused(pool, tensor, *operands):
    (
        hidden,
        input_gain,
        query_weight,
        key_weight,
        value_weight,
        query_gain,
        key_gain,
        output_weight,
        post_gain,
        gate_weight,
        up_weight,
        down_weight,
        key_cache,
        value_cache,
        lengths,
        request_slot,
    ) = operands
    devices = pool * tensor
    rows, width = hidden.shape
    head_dim = query_gain.shape[0]
    query_cols = query_weight.shape[1]
    key_cols = key_weight.shape[1]
    heads_here = query_cols // head_dim
    kv_count = devices * key_cols // head_dim
    per_kv = devices // kv_count
    requests = devices * rows
    half_width = head_dim // 2
    frequency = theta ** (-np.arange(half_width) * 2.0 / head_dim)
    frequency = np.concatenate([frequency, frequency])[None, :].astype(np.float32)
    heavy = (
        query_weight,
        key_weight.T,
        value_weight.T,
        output_weight,
        gate_weight.T,
        up_weight.T,
        down_weight,
        key_cache,
        value_cache,
    )
    dma = pltpu.SemaphoreType.DMA
    sent_cols = query_cols + head_dim
    sums = [
        pltpu.VMEM((SPLIT, pool, tensor * rows, width // SPLIT), BF16),
        pltpu.VMEM((SPLIT, tensor * rows, width // SPLIT), BF16),
        pltpu.VMEM((SPLIT, tensor, rows, width // SPLIT), BF16),
        pltpu.VMEM((SPLIT, tensor, rows, width // SPLIT), BF16),
    ]
    scratch = (
        [pltpu.VMEM(w.shape, w.dtype) for w in heavy]
        + [pltpu.VMEM((SPLIT, devices, rows, width // SPLIT), BF16)] * 2
        + [
            pltpu.VMEM((requests, width), F32),
            pltpu.VMEM((devices * SLOTS, sent_cols), F32),
            pltpu.VMEM((devices, SLOTS, sent_cols), BF16),
            pltpu.VMEM((devices, SLOTS, sent_cols), BF16),
            pltpu.VMEM((devices * heads_here * SLOTS, head_dim), F32),
            pltpu.VMEM((kv_count * 2 * SLOTS, per_kv * head_dim), F32),
            pltpu.VMEM((devices * heads_here * SLOTS, head_dim), F32),
            pltpu.VMEM((devices, SLOTS, query_cols), BF16),
            pltpu.VMEM((devices, SLOTS, query_cols), BF16),
            pltpu.VMEM((devices * SLOTS, query_cols), F32),
        ]
        + sums
        + sums
        + [dma((len(heavy),))]
        + [dma((SPLIT, 2 * tensor)), dma((SPLIT, devices))] * 2
        + [dma((devices,)), dma((devices,))] * 2
        + [dma((SPLIT, tensor)), dma((SPLIT, tensor + 1))] * 2
    )
    vmem = pl.BlockSpec(memory_space=pltpu.VMEM)
    hbm = pl.BlockSpec(memory_space=pl.ANY)
    row = jax.ShapeDtypeStruct(hidden.shape, F32)
    mixed, added = pl.pallas_call(
        functools.partial(step_kernel, pool, tensor),
        out_shape=(row, row),
        in_specs=[vmem] * 8 + [hbm] * len(heavy),
        out_specs=(vmem, vmem),
        scratch_shapes=scratch,
        compiler_params=pltpu.CompilerParams(
            collective_id=0, has_side_effects=True, vmem_limit_bytes=62 * 1024 * 1024
        ),
    )(
        hidden,
        input_gain[None, :],
        query_gain[None, :],
        key_gain[None, :],
        post_gain[None, :],
        lengths[None, :],
        request_slot[None, :],
        frequency,
        *heavy,
    )
    return mixed.astype(hidden.dtype), (mixed + added).astype(hidden.dtype)


def dispatch(pool, tensor, *operands):
    query_cols = operands[2].shape[1]
    key_cols = operands[3].shape[1]
    head_dim = operands[5].shape[0]
    whole_heads = query_cols % head_dim == 0 and head_dim % key_cols == 0
    lanes = operands[0].shape[1] % (SPLIT * 512) == 0
    if pool == 2 and lanes and whole_heads and 2 * key_cols <= head_dim:
        return fused(pool, tensor, *operands)
    return on_device(*operands)


def solution(mesh):
    placed = (
        P(("groups", "pool", "tensor"), None),
        P(),
        P(None, ("pool", "tensor")),
        P(None, ("pool", "tensor")),
        P(None, ("pool", "tensor")),
        P(),
        P(),
        P(("pool", "tensor"), None),
        P(),
        P(None, ("pool", "tensor")),
        P(None, ("pool", "tensor")),
        P(("pool", "tensor"), None),
        P(("groups", "pool", "tensor"), None),
        P(("groups", "pool", "tensor"), None),
        P("groups"),
        P("groups"),
    )
    return jax.shard_map(
        functools.partial(dispatch, mesh.shape["pool"], mesh.shape["tensor"]),
        mesh=mesh,
        in_specs=placed,
        out_specs=(P(("groups", "pool", "tensor"), None), P(("groups", "pool", "tensor"), None)),
        check_vma=False,
    )
```

profile of v0, /device:TPU:0, one launch (start us, length us, event | category | flops | bytes accessed | tf_op | source)
XLA Modules:
  0.0 57.8 jit_solution(1032067488145197562)
XLA Ops:
  0.6 55.6 %shard_map.176 = (f32[2,5120]{1,0:T(2,128)}, f32[2,5120]{1,0:T(2,128)}) custom-call(bf16[2,5120]{1,0:T(2,128)(2,1)} %hidden_ref.1, f32[1,5120]{1,0:T(1,128)} %bitcast.14, f32[1,128]{1,0:T(1,128)} %bitcast.16, f32[1,128]{1,0:T(1,128)} %bitcast.17, f32[1,5120]{1,0:T(1,128)} %bitcast.15, s32[1,32]{1,0:T(1,128)} %bitcast.18, s32[1,32]{1,0:T(1,128)} %bitcast.19, ...), custom_call_target="tpu_custom_call" | custom-call | tf_op jit(solution)/shard_map/pallas_call | solution.py:730
  56.3 1.5 %add_convert_fusion = (bf16[2,5120]{1,0:T(2,128)(2,1)}, bf16[2,5120]{1,0:T(2,128)(2,1)}) fusion(f32[2,5120]{1,0:T(2,128)} %get-tuple-element.4, f32[2,5120]{1,0:T(2,128)} %get-tuple-element.5), kind=kLoop, calls=%fused_computation | loop fusion | flops 30720 | bytes 122880 | tf_op jit(solution)/shard_map/convert_element_type | solution.py:750
where the time goes:
time: 58 us; the launch traced here: 57.8 us
  Pallas kernels  55.6 us (96%)
  other arithmetic  1.51 us (3%)
  between operations  0.64 us (1%)
    pallas_call x1, Pallas kernels, fused(): pl.pallas_call(functools.partial(step_kernel, pool, tensor), out_shape=(r...  55.6 us
    convert_element_type x1, other arithmetic, fused(): return (mixed.astype(hidden.dtype), (mixed + added).astype(hidden.dtype))  1.51 us

commit v1 on v0

v1 whole, which is shorter than its diff:
```python
import functools
import math

import jax
import jax.numpy as jnp
import numpy as np
from jax import lax
from jax.experimental import pallas as pl
from jax.experimental.pallas import tpu as pltpu
from jax.sharding import PartitionSpec as P

SLOTS = 4


eps = 1e-06
theta = 1000000.0


def rms_scale(values, scales):
    values = values.astype(jnp.float32)
    return values * lax.rsqrt(jnp.mean(values * values, axis=-1, keepdims=True) + eps) * scales


def rotate(values, position):
    half_width = values.shape[-1] // 2
    frequency = theta ** (-jnp.arange(half_width, dtype=jnp.float32) * 2.0 / values.shape[-1])
    angles = position * frequency
    cosine = jnp.cos(angles)
    sine_part = jnp.sin(angles)
    front_half = values[..., :half_width]
    back_half = values[..., half_width:]
    return jnp.concatenate(
        [front_half * cosine - back_half * sine_part, back_half * cosine + front_half * sine_part],
        axis=-1,
    )


def on_device(
    hidden,
    input_gain,
    query_weight,
    key_weight,
    value_weight,
    query_gain,
    key_gain,
    output_weight,
    post_gain,
    gate_weight,
    up_weight,
    down_weight,
    key_cache,
    value_cache,
    lengths,
    request_slot,
):
    devices = lax.axis_size(("pool", "tensor"))
    device_index = lax.axis_index(("pool", "tensor"))
    local_rows = hidden.shape[0]
    query_cols = query_weight.shape[1]
    key_cols = key_weight.shape[1]
    width_sent = query_cols + 2 * key_cols
    head_dim = query_gain.shape[0]
    slot_count = SLOTS
    head_count = devices * query_cols // head_dim
    kv_count = devices * key_cols // head_dim
    group_size = head_count // kv_count
    normed = rms_scale(hidden, input_gain).astype(jnp.bfloat16)
    shard_rows = lax.all_gather(normed, ("pool", "tensor"), axis=0, tiled=True)
    query_part = jnp.dot(shard_rows, query_weight, preferred_element_type=jnp.float32)
    key_part = jnp.dot(shard_rows, key_weight, preferred_element_type=jnp.float32)
    value_part = jnp.dot(shard_rows, value_weight, preferred_element_type=jnp.float32)
    projected = jnp.concatenate([query_part, key_part, value_part], axis=1).astype(jnp.bfloat16)
    outgoing = (
        jnp.zeros((devices * slot_count, width_sent), jnp.bfloat16).at[request_slot].set(projected)
    )
    outgoing = outgoing.reshape(devices, slot_count, width_sent)
    arrived = lax.all_to_all(
        outgoing, ("pool", "tensor"), split_axis=0, concat_axis=2, tiled=True
    ).reshape(slot_count, devices, width_sent)
    query_full = arrived[:, :, :query_cols].reshape(slot_count, head_count, head_dim)
    key_full = arrived[:, :, query_cols : query_cols + key_cols].reshape(
        slot_count, kv_count, head_dim
    )
    value_new = arrived[:, :, query_cols + key_cols :].reshape(slot_count, kv_count, head_dim)
    slot_ids = device_index * slot_count + jnp.arange(slot_count, dtype=jnp.int32)
    matches = request_slot[None, :] == slot_ids[:, None]
    slot_length = jnp.sum(jnp.where(matches, lengths[None, :], 0), axis=1)
    owner_of = request_slot // slot_count
    within = request_slot % slot_count
    earlier = (owner_of[None, :] == device_index) & (
        within[None, :] < jnp.arange(slot_count, dtype=jnp.int32)[:, None]
    )
    slot_offset = jnp.sum(jnp.where(earlier, lengths[None, :], 0), axis=1)
    position = slot_length.astype(jnp.float32)[:, None, None]
    query_heads = rotate(rms_scale(query_full, query_gain), position).astype(jnp.bfloat16)
    query_heads = query_heads.reshape(slot_count, kv_count, group_size, head_dim)
    key_new = rotate(rms_scale(key_full, key_gain), position).astype(jnp.bfloat16)
    pool_tokens = key_cache.shape[0]
    cached_keys = key_cache.reshape(pool_tokens, kv_count, head_dim)
    cached_values = value_cache.reshape(pool_tokens, kv_count, head_dim)
    scale_factor = 1.0 / math.sqrt(head_dim)
    scores = (
        jnp.einsum("skgd,tkd->skgt", query_heads, cached_keys, preferred_element_type=jnp.float32)
        * scale_factor
    )
    own_score = (
        jnp.einsum("skgd,skd->skg", query_heads, key_new, preferred_element_type=jnp.float32)
        * scale_factor
    )
    token_pos = jnp.arange(pool_tokens, dtype=jnp.int32)
    inside = (token_pos[None, :] >= slot_offset[:, None]) & (
        token_pos[None, :] < (slot_offset + slot_length)[:, None]
    )
    inside = inside[:, None, None, :]
    largest = jnp.maximum(jnp.max(jnp.where(inside, scores, -1e30), axis=3), own_score)
    weights = jnp.where(inside, jnp.exp(scores - largest[..., None]), 0.0)
    own_weight = jnp.exp(own_score - largest)
    denominator = jnp.sum(weights, axis=3) + own_weight
    summed = jnp.einsum(
        "skgt,tkd->skgd",
        weights.astype(jnp.bfloat16),
        cached_values,
        preferred_element_type=jnp.float32,
    )
    own_low = own_weight.astype(jnp.bfloat16).astype(jnp.float32)
    summed = summed + own_low[..., None] * value_new.astype(jnp.float32)[:, :, None, :]
    head_out = (
        (summed / denominator[..., None])
        .astype(jnp.bfloat16)
        .reshape(slot_count, devices, query_cols)
    )
    returned = lax.all_to_all(head_out, ("pool", "tensor"), split_axis=1, concat_axis=0, tiled=True)
    head_rows = returned.reshape(devices * slot_count, query_cols)[request_slot]
    partial_value = jnp.dot(head_rows, output_weight, preferred_element_type=jnp.float32)
    row_start = device_index * local_rows
    own_part = lax.dynamic_slice_in_dim(partial_value, row_start, local_rows, 0) + hidden.astype(
        jnp.float32
    )
    partial_value = lax.dynamic_update_slice_in_dim(partial_value, own_part, row_start, 0)
    totals = lax.psum(partial_value, ("pool", "tensor"))
    mixed_all = totals.astype(jnp.bfloat16)
    mixed_rows = lax.dynamic_slice_in_dim(mixed_all, row_start, local_rows, 0)
    post_normed = rms_scale(mixed_all, post_gain).astype(jnp.bfloat16)
    gate_part = jnp.dot(post_normed, gate_weight, preferred_element_type=jnp.float32)
    up_part = jnp.dot(post_normed, up_weight, preferred_element_type=jnp.float32)
    activated = (jax.nn.silu(gate_part) * up_part).astype(jnp.bfloat16)
    lowered = lax.psum_scatter(
        jnp.dot(activated, down_weight, preferred_element_type=jnp.float32),
        ("pool", "tensor"),
        scatter_dimension=0,
        tiled=True,
    )
    final_rows = (mixed_rows.astype(jnp.float32) + lowered).astype(jnp.bfloat16)
    return (mixed_rows, final_rows)


MESH = pl.DeviceIdType.MESH
F32 = jnp.float32
BF16 = jnp.bfloat16


def step_kernel(
    pool,
    tensor,
    hidden_ref,
    input_gain_ref,
    query_gain_ref,
    key_gain_ref,
    post_gain_ref,
    length_ref,
    slot_ref,
    frequency_ref,
    qw_hbm,
    kw_hbm,
    vw_hbm,
    ow_hbm,
    gw_hbm,
    uw_hbm,
    dw_hbm,
    kc_hbm,
    vc_hbm,
    mixed_ref,
    final_ref,
    qw,
    kvw,
    ow,
    gw,
    uw,
    dw,
    kc,
    vc,
    ag1,
    hid,
    hblock,
    xs,
    to_owner,
    at_owner,
    to_home,
    at_home,
    part1,
    peer1,
    out1,
    in1,
    mb,
    part2,
    peer2,
    sum2,
    out2,
    in2,
    load_sem,
    ag1_s,
    ag1_r,
    hid_s,
    hid_r,
    ag2_s,
    ag2_r,
    a1_s,
    a1_r,
    a2_s,
    a2_r,
    sw1_s,
    sw1_r,
    rs1_s,
    rs1_r,
    sw2_s,
    sw2_r,
    rs2_s,
    rs2_r,
):
    devices = pool * tensor
    rows, width = hidden_ref.shape
    requests = devices * rows
    half = tensor * rows
    block = width // tensor
    head_dim = query_gain_ref.shape[1]
    query_cols = qw.shape[1]
    key_cols = kvw.shape[0] // 2
    heads_here = query_cols // head_dim
    head_count = devices * heads_here
    kv_count = devices * key_cols // head_dim
    per_kv = devices // kv_count
    group = head_count // kv_count
    hidden_units = gw.shape[0]
    pieces = heads_here + 2
    span = 2 * SLOTS
    p = lax.axis_index("pool")
    t = lax.axis_index("tensor")
    me = p * tensor + t
    partner = {"pool": 1 - p, "tensor": t}

    barrier = pltpu.get_barrier_semaphore()

    def place(index):
        return {"pool": lax.div(index, tensor), "tensor": lax.rem(index, tensor)}

    for j in range(1, devices):
        pl.semaphore_signal(
            barrier, inc=1, device_id=place(lax.rem(me + j, devices)), device_id_type=MESH
        )

    loads = [
        pltpu.make_async_copy(a, b, load_sem.at[i])
        for i, (a, b) in enumerate(
            [
                (qw_hbm, qw),
                (kw_hbm, kvw.at[:key_cols]),
                (vw_hbm, kvw.at[key_cols:]),
                (kc_hbm, kc),
                (vc_hbm, vc),
                (ow_hbm, ow),
                (gw_hbm, gw),
                (uw_hbm, uw),
                (dw_hbm, dw),
            ]
        )
    ]
    for load in loads:
        load.start()

    def flip(j):
        out, bit = 0, 1
        while bit < tensor:
            digit = lax.rem(lax.div(t, bit), 2)
            out = out + bit * (1 - digit if (j // bit) % 2 else digit)
            bit *= 2
        return out

    near = [flip(j) for j in range(tensor)]
    around = range(1, tensor)

    def remote(source, target, sent, received, where):
        return pltpu.make_async_remote_copy(
            src_ref=source,
            dst_ref=target,
            send_sem=sent,
            recv_sem=received,
            device_id=where,
            device_id_type=MESH,
        )

    def in_plane(other):
        return {"pool": p, "tensor": other}

    class Gather:
        def __init__(self, buffer, sent, received):
            self.buffer, self.sent, self.received = buffer, sent, received

        def slot(self, q, index, k, where):
            at = self.buffer.at[q, index]
            return remote(at, at, self.sent.at[k], self.received.at[q, index], where)

        def send(self):
            for j in around:
                self.slot(p, t, j, in_plane(near[j])).start()
            self.slot(p, t, 0, partner).start()

        def forward(self, j):
            self.slot(p, near[j], tensor + j, partner).wait_recv()
            self.slot(p, near[j], tensor + j, partner).start()

        def across(self, j):
            self.slot(1 - p, near[j], 0, partner).wait_recv()

        def finish(self):
            self.slot(p, t, 0, partner).wait_send()
            for j in around:
                self.slot(p, t, j, in_plane(near[j])).wait_send()
                self.slot(p, near[j], tensor + j, partner).wait_send()

    first = Gather(ag1, ag1_s, ag1_r)
    second = Gather(mb, ag2_s, ag2_r)

    def hidden_copy(j, index):
        lanes = pl.ds(pl.multiple_of(near[j] * block, block), block)
        return remote(
            hidden_ref.at[:, lanes], hid.at[index], hid_s.at[j], hid_r.at[index], in_plane(near[j])
        )

    hidden = hidden_ref[...].astype(F32)
    ag1[p, t] = rms_scale(hidden, input_gain_ref[...]).astype(BF16)

    slot_row = slot_ref[...]
    length_row = length_ref[...]

    def iota(shape, dim):
        return lax.broadcasted_iota(jnp.int32, shape, dim)

    def hot(mask):
        return mask.astype(F32).astype(BF16)

    spread = hot(iota((requests, pieces * requests), 0) == lax.rem(iota((requests, pieces * requests), 1), requests))
    slot_wide = jnp.broadcast_to(slot_row, (span, requests))
    slot_tiled = jnp.dot(
        slot_wide.astype(F32).astype(BF16), spread, preferred_element_type=F32
    ).astype(jnp.int32)[:1]
    tall = devices * pieces * SLOTS
    row = iota((tall, pieces * requests), 0)
    col = iota((tall, pieces * requests), 1)
    wanted = lax.div(row, pieces * SLOTS) * SLOTS + lax.rem(row, SLOTS)
    scatter_hot = hot(
        (lax.rem(lax.div(row, SLOTS), pieces) == lax.div(col, requests)) & (wanted == slot_tiled)
    )
    eye = iota((requests, requests), 0) == iota((requests, requests), 1)
    slot_col = jnp.sum(
        jnp.where(eye, jnp.broadcast_to(slot_row, (requests, requests)), 0).astype(F32),
        axis=1,
        keepdims=True,
    ).astype(jnp.int32)
    home = devices * heads_here * SLOTS
    col = iota((requests, home), 1)
    held = lax.div(col, heads_here * SLOTS) * SLOTS + lax.rem(col, SLOTS)
    which = lax.rem(lax.div(col, SLOTS), heads_here)
    gather_hot = jnp.concatenate(
        [hot((which == i) & (held == slot_col)) for i in range(heads_here)], axis=0
    )
    place_id = lax.rem(iota((span, requests), 0), SLOTS)
    length_wide = jnp.broadcast_to(length_row, (span, requests)).astype(F32)
    base = me * SLOTS
    slot_length = jnp.sum(
        jnp.where(slot_wide == base + place_id, length_wide, 0.0), axis=1, keepdims=True
    )
    slot_offset = jnp.sum(
        jnp.where((slot_wide >= base) & (slot_wide < base + place_id), length_wide, 0.0),
        axis=1,
        keepdims=True,
    )
    angles = slot_length * frequency_ref[...]
    cosine = jnp.cos(angles)
    lane = iota((span, head_dim), 1)
    sine_part = jnp.where(lane < head_dim // 2, -jnp.sin(angles), jnp.sin(angles))
    pool_tokens = kc.shape[0]
    token = iota((span, pool_tokens), 1).astype(F32)
    inside = jnp.where((token >= slot_offset) & (token < slot_offset + slot_length), 1.0, 0.0)

    def turn(values, scale, copies):
        scaled = rms_scale(values, scale)
        return scaled * jnp.tile(cosine, (copies, 1)) + pltpu.roll(
            scaled, head_dim // 2, 1
        ) * jnp.tile(sine_part, (copies, 1))

    def turned(left, weight):
        return lax.dot_general(left, weight, (((1,), (1,)), ((), ())), preferred_element_type=F32)

    pl.semaphore_wait(barrier, devices - 1)
    first.send()
    for j in around:
        hidden_copy(j, t).start()
    hid[t] = hidden_ref[:, pl.ds(pl.multiple_of(t * block, block), block)]
    for load in loads[:3]:
        load.wait()
    for j in around:
        first.forward(j)
    for index in range(tensor):
        xs[p, index * rows : (index + 1) * rows, :] = ag1[p, index].astype(F32)
    for j in range(tensor):
        first.across(j)
    for index in range(tensor):
        xs[1 - p, index * rows : (index + 1) * rows, :] = ag1[1 - p, index].astype(F32)

    left = jnp.concatenate([xs[q] for q in range(pool)], axis=0).astype(BF16)
    query_part = jnp.dot(left, qw[...], preferred_element_type=F32).astype(BF16)
    kv_part = turned(left, kvw[...]).astype(BF16)

    wide = iota((2 * key_cols, 2 * head_dim), 1)
    tall = iota((2 * key_cols, 2 * head_dim), 0)
    shift = lax.rem(me, per_kv) * key_cols
    aim = jnp.where(tall < key_cols, tall + shift, tall - key_cols + head_dim + shift)
    kv_wide = jnp.dot(kv_part, hot(aim == wide), preferred_element_type=F32).astype(BF16)
    stacked = jnp.concatenate(
        [query_part[:, i * head_dim : (i + 1) * head_dim] for i in range(heads_here)]
        + [kv_wide[:, :head_dim], kv_wide[:, head_dim:]],
        axis=0,
    )
    slots = jnp.dot(scatter_hot, stacked, preferred_element_type=F32).astype(BF16)
    deep = pieces * SLOTS
    for index in range(devices):
        to_owner[index] = slots[index * deep : (index + 1) * deep]

    def exchange(outgoing, incoming, sent, received):
        def copy(j, index):
            peer = lax.rem(me + j, devices)
            slot = peer if index is None else index
            return remote(
                outgoing.at[peer], incoming.at[slot], sent.at[j], received.at[slot], place(peer)
            )

        for j in range(1, devices):
            copy(j, me).start()
        incoming[me] = outgoing[me]

        def arrive():
            for j in range(1, devices):
                copy(j, None).wait_recv()

        def finish():
            for j in range(1, devices):
                copy(j, me).wait_send()

        return arrive, finish

    arrive, sent_a1 = exchange(to_owner, at_owner, a1_s, a1_r)

    for j in around:
        hidden_copy(j, near[j]).wait_recv()
    for index in range(tensor):
        hblock[index * rows : (index + 1) * rows, :] = hid[index].astype(F32)
    for load in loads[3:5]:
        load.wait()
    arrive()

    scale_factor = 1.0 / math.sqrt(head_dim)
    copies = group * SLOTS // span
    allowed = jnp.tile(inside, (copies, 1)) > 0.5
    upper = iota((span, head_dim), 0) < SLOTS
    deep = heads_here * SLOTS
    for k in range(kv_count):
        blocks = [at_owner[k * per_kv + j].astype(F32) for j in range(per_kv)]
        query = jnp.concatenate([b[:deep] for b in blocks], axis=0)
        both = blocks[0][deep:]
        for b in blocks[1:]:
            both = both + b[deep:]
        turned_over = pltpu.roll(both, SLOTS, 0)
        key_new = turn(jnp.where(upper, both, turned_over), key_gain_ref[...], 1)
        own_value = jnp.tile(jnp.where(upper, turned_over, both), (copies, 1))
        own_key = jnp.tile(key_new.astype(BF16).astype(F32), (copies, 1))
        query = turn(query, query_gain_ref[...], copies).astype(BF16)
        lanes = slice(k * head_dim, (k + 1) * head_dim)
        scores = turned(query, kc[:, lanes]) * scale_factor
        own_score = jnp.sum(query.astype(F32) * own_key, axis=1, keepdims=True) * scale_factor
        scores = jnp.where(allowed, scores, -1e30)
        largest = jnp.maximum(jnp.max(scores, axis=1, keepdims=True), own_score)
        weights = jnp.exp(scores - largest)
        own_weight = jnp.exp(own_score - largest)
        denominator = jnp.sum(weights, axis=1, keepdims=True) + own_weight
        summed = jnp.dot(weights.astype(BF16), vc[:, lanes], preferred_element_type=F32)
        summed = summed + own_weight.astype(BF16).astype(F32) * own_value
        head_out = summed / denominator
        for j in range(per_kv):
            to_home[k * per_kv + j] = head_out[j * deep : (j + 1) * deep]

    arrive, sent_a2 = exchange(to_home, at_home, a2_s, a2_r)
    loads[5].wait()
    arrive()
    back = jnp.concatenate([at_home[index] for index in range(devices)], axis=0).astype(BF16)
    gathered = jnp.dot(gather_hot, back, preferred_element_type=F32).astype(BF16)
    head_rows = jnp.concatenate(
        [gathered[i * requests : (i + 1) * requests] for i in range(heads_here)], axis=1
    )

    pairs = tensor // 2
    wide = 2 * block

    def swap(part, peer, sent, received, c):
        return remote(part.at[c, 1 - p], peer.at[c], sent.at[c], received.at[c], partner)

    def products(left, weight, part, peer, sent, received, order):
        for c in range(pairs):
            at = pl.ds(pl.multiple_of(order[c] * wide, wide), wide)
            product = jnp.dot(left, weight[:, at], preferred_element_type=F32)
            for q in range(pool):
                part[c, q] = product[q * half : (q + 1) * half].astype(BF16)
            swap(part, peer, sent, received, c).start()

    turn_of = [lax.rem(lax.div(t, 2) + 1 + c, pairs) for c in range(pairs)]
    products(head_rows, ow, part1, peer1, sw1_s, sw1_r, turn_of)

    def block_copy(k, other, slot):
        return remote(out1.at[other], in1.at[slot], rs1_s.at[k], rs1_r.at[slot], in_plane(other))

    for c in range(pairs):
        swap(part1, peer1, sw1_s, sw1_r, c).wait_recv()
        total = (peer1[c].astype(F32) + part1[c, p].astype(F32)).astype(BF16)
        for i in range(2):
            out1[2 * turn_of[c] + i] = total[:, i * block : (i + 1) * block]
        if c + 1 < pairs:
            for i in range(2):
                block_copy(2 * c + i, 2 * turn_of[c] + i, t).start()
    block_copy(tensor - 2, near[1], t).start()
    total = hblock[...] + out1[t].astype(F32)
    for j in around:
        block_copy(0, near[j], near[j]).wait_recv()
        total = total + in1[near[j]].astype(F32)
    mb[p, t] = total.astype(BF16)
    second.send()

    def part_of(j):
        at = pl.ds(pl.multiple_of(near[j] * block, block), block)
        values = jnp.concatenate([mb[q, near[j]] for q in range(pool)], axis=0).astype(F32)
        squares = values * values
        some = squares[:, :128]
        for i in range(1, block // 128):
            some = some + squares[:, i * 128 : (i + 1) * 128]
        scaled = (values * post_gain_ref[:, at]).astype(BF16)
        return some, turned(scaled, gw[:, at]), turned(scaled, uw[:, at])

    loads[6].wait()
    loads[7].wait()
    lead = 2
    sent_up_to = 0
    acc = None
    for j in range(tensor):
        while sent_up_to < min(j + lead, tensor - 1) and j > 0 or sent_up_to < j:
            sent_up_to += 1
            second.forward(sent_up_to)
        second.across(j)
        new = part_of(j)
        acc = new if acc is None else tuple(a + b for a, b in zip(acc, new))
    square, gate_part, up_part = acc
    mean = jnp.sum(square, axis=1, keepdims=True) * (1.0 / width)
    scale = lax.rsqrt(mean + eps)
    gate_part = gate_part * scale
    up_part = up_part * scale
    activated = (gate_part / (1.0 + jnp.exp(-gate_part)) * up_part).astype(BF16)

    loads[8].wait()
    products(activated, dw, part2, peer2, sw2_s, sw2_r, list(range(pairs)))

    def row_copy(c, j, slot):
        lanes = slice(c * wide, (c + 1) * wide)
        return remote(
            out2.at[near[j], :, lanes],
            in2.at[slot, :, lanes],
            rs2_s.at[c, j],
            rs2_r.at[c, slot],
            in_plane(near[j]),
        )

    for c in range(pairs):
        lanes = slice(c * wide, (c + 1) * wide)
        swap(part2, peer2, sw2_s, sw2_r, c).wait_recv()
        sum2[:, lanes] = peer2[c].astype(F32) + part2[c, p].astype(F32)
        for index in range(tensor):
            out2[index, :, lanes] = sum2[index * rows : (index + 1) * rows, lanes].astype(BF16)
        for j in around:
            row_copy(c, j, t).start()

    pick = hot(iota((8, requests), 1) == me * rows + iota((8, requests), 0))
    mixed = jnp.concatenate(
        [
            jnp.dot(
                pick,
                jnp.concatenate([mb[q, index] for q in range(pool)], axis=0),
                preferred_element_type=F32,
            )[:rows]
            for index in range(tensor)
        ],
        axis=1,
    )
    mixed_ref[...] = mixed.astype(BF16)
    first.finish()
    sent_a1()
    sent_a2()
    second.finish()
    for j in around:
        hidden_copy(j, t).wait_send()
    for c in range(pairs):
        swap(part1, peer1, sw1_s, sw1_r, c).wait_send()
        swap(part2, peer2, sw2_s, sw2_r, c).wait_send()
    for c in range(pairs - 1):
        for i in range(2):
            block_copy(2 * c + i, 2 * turn_of[c] + i, t).wait_send()
    block_copy(tensor - 2, near[1], t).wait_send()

    for c in range(pairs):
        lanes = slice(c * wide, (c + 1) * wide)
        total = mixed[:, lanes]
        lowered = out2[t, :, lanes].astype(F32)
        for j in around:
            row_copy(c, j, near[j]).wait_recv()
            lowered = lowered + in2[near[j], :, lanes].astype(F32)
        final_ref[:, lanes] = (total + lowered).astype(BF16)
    for c in range(pairs):
        for j in around:
            row_copy(c, j, t).wait_send()


def fused(pool, tensor, *operands):
    (
        hidden,
        input_gain,
        query_weight,
        key_weight,
        value_weight,
        query_gain,
        key_gain,
        output_weight,
        post_gain,
        gate_weight,
        up_weight,
        down_weight,
        key_cache,
        value_cache,
        lengths,
        request_slot,
    ) = operands
    devices = pool * tensor
    rows, width = hidden.shape
    head_dim = query_gain.shape[0]
    query_cols = query_weight.shape[1]
    key_cols = key_weight.shape[1]
    heads_here = query_cols // head_dim
    half = tensor * rows
    block = width // tensor
    pairs = tensor // 2
    half_width = head_dim // 2
    frequency = theta ** (-np.arange(half_width) * 2.0 / head_dim)
    frequency = np.concatenate([frequency, frequency])[None, :].astype(np.float32)
    gate_turned, up_turned = gate_weight.T, up_weight.T
    dma = pltpu.SemaphoreType.DMA
    deep = (heads_here + 2) * SLOTS
    scratch = [
        pltpu.VMEM(query_weight.shape, BF16),
        pltpu.VMEM((2 * key_cols, width), BF16),
        pltpu.VMEM(output_weight.shape, BF16),
        pltpu.VMEM(gate_turned.shape, BF16),
        pltpu.VMEM(up_turned.shape, BF16),
        pltpu.VMEM(down_weight.shape, BF16),
        pltpu.VMEM(key_cache.shape, BF16),
        pltpu.VMEM(value_cache.shape, BF16),
        pltpu.VMEM((pool, tensor, rows, width), BF16),
        pltpu.VMEM((tensor, rows, block), BF16),
        pltpu.VMEM((half, block), F32),
        pltpu.VMEM((pool, half, width), F32),
        pltpu.VMEM((devices, deep, head_dim), BF16),
        pltpu.VMEM((devices, deep, head_dim), BF16),
        pltpu.VMEM((devices, heads_here * SLOTS, head_dim), F32),
        pltpu.VMEM((devices, heads_here * SLOTS, head_dim), F32),
        pltpu.VMEM((pairs, pool, half, 2 * block), BF16),
        pltpu.VMEM((pairs, half, 2 * block), BF16),
        pltpu.VMEM((tensor, half, block), BF16),
        pltpu.VMEM((tensor, half, block), BF16),
        pltpu.VMEM((pool, tensor, half, block), BF16),
        pltpu.VMEM((pairs, pool, half, 2 * block), BF16),
        pltpu.VMEM((pairs, half, 2 * block), BF16),
        pltpu.VMEM((half, width), F32),
        pltpu.VMEM((tensor, rows, width), BF16),
        pltpu.VMEM((tensor, rows, width), BF16),
        dma((9,)),
        dma((2 * tensor,)),
        dma((pool, tensor)),
        dma((tensor,)),
        dma((tensor,)),
        dma((2 * tensor,)),
        dma((pool, tensor)),
        dma((devices,)),
        dma((devices,)),
        dma((devices,)),
        dma((devices,)),
        dma((pairs,)),
        dma((pairs,)),
        dma((tensor,)),
        dma((tensor,)),
        dma((pairs,)),
        dma((pairs,)),
        dma((pairs, tensor)),
        dma((pairs, tensor)),
    ]
    vmem = pl.BlockSpec(memory_space=pltpu.VMEM)
    hbm = pl.BlockSpec(memory_space=pl.ANY)
    row = jax.ShapeDtypeStruct(hidden.shape, BF16)
    return pl.pallas_call(
        functools.partial(step_kernel, pool, tensor),
        out_shape=(row, row),
        in_specs=[vmem] * 8 + [hbm] * 9,
        out_specs=(vmem, vmem),
        scratch_shapes=scratch,
        compiler_params=pltpu.CompilerParams(
            collective_id=0, has_side_effects=True, vmem_limit_bytes=62 * 1024 * 1024
        ),
    )(
        hidden,
        input_gain[None, :],
        query_gain[None, :],
        key_gain[None, :],
        post_gain[None, :],
        lengths[None, :],
        request_slot[None, :],
        frequency,
        query_weight,
        key_weight.T,
        value_weight.T,
        output_weight,
        gate_turned,
        up_turned,
        down_weight,
        key_cache,
        value_cache,
    )


def dispatch(pool, tensor, *operands):
    rows, width = operands[0].shape
    query_cols = operands[2].shape[1]
    key_cols = operands[3].shape[1]
    head_dim = operands[5].shape[0]
    devices = pool * tensor
    lanes = width % (tensor * 128) == 0 and head_dim == 128
    paired = tensor >= 4 and tensor & (tensor - 1) == 0 and tensor * rows == 16
    heads = query_cols == 2 * head_dim and head_dim % key_cols == 0
    few = devices * SLOTS <= 256 and devices * rows * 4 % 128 == 0
    if pool == 2 and lanes and paired and heads and few:
        return fused(pool, tensor, *operands)
    return on_device(*operands)


def solution(mesh):
    placed = (
        P(("groups", "pool", "tensor"), None),
        P(),
        P(None, ("pool", "tensor")),
        P(None, ("pool", "tensor")),
        P(None, ("pool", "tensor")),
        P(),
        P(),
        P(("pool", "tensor"), None),
        P(),
        P(None, ("pool", "tensor")),
        P(None, ("pool", "tensor")),
        P(("pool", "tensor"), None),
        P(("groups", "pool", "tensor"), None),
        P(("groups", "pool", "tensor"), None),
        P("groups"),
        P("groups"),
    )
    return jax.shard_map(
        functools.partial(dispatch, mesh.shape["pool"], mesh.shape["tensor"]),
        mesh=mesh,
        in_specs=placed,
        out_specs=(P(("groups", "pool", "tensor"), None), P(("groups", "pool", "tensor"), None)),
        check_vma=False,
    )
```

time: 58 us -> 56 us (0.966)
  Pallas kernels: 55.6 us -> 52.4 us
  local copies, waits for them, and re-layouts: 0 us -> 2.7 us
  other arithmetic: 1.51 us -> 0 us
    pallas_call x1, Pallas kernels: 55.6 us -> 52.4 us  [fused(): pl.pallas_call(functools.partial(step_kernel, pool, tensor), out_shape=(r...]
    unnamed x0 -> x2, local copies, waits for them, and re-layouts: none -> 2.7 us
    convert_element_type x1 -> x0, other arithmetic: 1.51 us -> none  [fused(): return (mixed.astype(hidden.dtype), (mixed + added).astype(hidden.dtype))]
where the time goes in v1:
time: 56 us; the launch traced here: 55.7 us
  Pallas kernels  52.4 us (94%)
  local copies, waits for them, and re-layouts  2.7 us (5%)
  between operations  0.65 us (1%)
    pallas_call x1, Pallas kernels, fused(): pl.pallas_call(functools.partial(step_kernel, pool, tensor), out_shape=(r...  52.4 us
    unnamed x2, local copies, waits for them, and re-layouts  2.7 us

profile of v1, /device:TPU:0, one launch (start us, length us, event | category | flops | bytes accessed | tf_op | source)
XLA Modules:
  0.0 55.7 jit_solution(13051484082540989136)
XLA Ops:
  0.6 52.4 %shard_map.176 = (bf16[2,5120]{1,0:T(2,128)(2,1)}, bf16[2,5120]{1,0:T(2,128)(2,1)}) custom-call(bf16[2,5120]{1,0:T(2,128)(2,1)} %hidden_ref.1, f32[1,5120]{1,0:T(1,128)} %bitcast.14, f32[1,128]{1,0:T(1,128)} %bitcast.16, f32[1,128]{1,0:T(1,128)} %bitcast.17, f32[1,5120]{1,0:T(1,128)} %bitcast.15, s32[1,32]{1,0:T(1,128)} %bitcast.18, s32[1,32]{1,0:T(1,128)} %bitcast.19, ...), custom_call_target="tpu_custom_call" | custom-call | tf_op jit(solution)/shard_map/pallas_call | solution.py:721
  53.0 1.3 %copy.21 = bf16[2,5120]{1,0:T(2,128)(2,1)} copy(bf16[2,5120]{1,0:T(2,128)(2,1)} %get-tuple-element.4) | data formatting | bytes 40960
  54.4 1.3 %copy.22 = bf16[2,5120]{1,0:T(2,128)(2,1)} copy(bf16[2,5120]{1,0:T(2,128)(2,1)} %get-tuple-element.5) | data formatting | bytes 40960

commit v2 on v1

--- a/solution.py
+++ b/solution.py
@@ -157,19 +157,20 @@
 MESH = pl.DeviceIdType.MESH
 F32 = jnp.float32
 BF16 = jnp.bfloat16
+CUTS = 2
 
 
 def step_kernel(
     pool,
     tensor,
-    hidden_ref,
-    input_gain_ref,
-    query_gain_ref,
-    key_gain_ref,
-    post_gain_ref,
-    length_ref,
-    slot_ref,
-    frequency_ref,
+    hidden_hbm,
+    slot_hbm,
+    length_hbm,
+    input_gain_hbm,
+    frequency_hbm,
+    query_gain_hbm,
+    key_gain_hbm,
+    post_gain_hbm,
     qw_hbm,
     kw_hbm,
     vw_hbm,
@@ -180,7 +181,15 @@
     kc_hbm,
     vc_hbm,
     mixed_ref,
-    final_ref,
+    added_ref,
+    hidden_ref,
+    slot_ref,
+    length_ref,
+    input_gain_ref,
+    frequency_ref,
+    query_gain_ref,
+    key_gain_ref,
+    post_gain_ref,
     qw,
     kvw,
     ow,
@@ -207,6 +216,7 @@
     sum2,
     out2,
     in2,
+    small_sem,
     load_sem,
     ag1_s,
     ag1_r,
@@ -258,6 +268,24 @@
             barrier, inc=1, device_id=place(lax.rem(me + j, devices)), device_id_type=MESH
         )
 
+    smalls = [
+        pltpu.make_async_copy(a, b, small_sem.at[i])
+        for i, (a, b) in enumerate(
+            [
+                (hidden_hbm, hidden_ref),
+                (slot_hbm, slot_ref),
+                (length_hbm, length_ref),
+                (input_gain_hbm, input_gain_ref),
+                (frequency_hbm, frequency_ref),
+                (query_gain_hbm, query_gain_ref),
+                (key_gain_hbm, key_gain_ref),
+                (post_gain_hbm, post_gain_ref),
+            ]
+        )
+    ]
+    for load in smalls:
+        load.start()
+
     loads = [
         pltpu.make_async_copy(a, b, load_sem.at[i])
         for i, (a, b) in enumerate(
@@ -274,8 +302,6 @@
             ]
         )
     ]
-    for load in loads:
-        load.start()
 
     def flip(j):
         out, bit = 0, 1
@@ -285,8 +311,15 @@
             bit *= 2
         return out
 
-    near = [flip(j) for j in range(tensor)]
     around = range(1, tensor)
+    spin = [lax.rem(t + j, tensor) for j in range(tensor)]
+    if tensor == 8:
+        deep, side = lax.div(t, 2), lax.rem(t, 2)
+        upper = lax.div(deep, 2)
+        layers = [deep, deep + 1 - 2 * lax.rem(deep, 2), 2 - upper, 3 - 3 * upper]
+        near = [2 * layer + q for layer in layers for q in (side, 1 - side)]
+    else:
+        near = [flip(j) for j in range(tensor)]
 
     def remote(source, target, sent, received, where):
         return pltpu.make_async_remote_copy(
@@ -311,7 +344,7 @@
 
         def send(self):
             for j in around:
-                self.slot(p, t, j, in_plane(near[j])).start()
+                self.slot(p, t, j, in_plane(spin[j])).start()
             self.slot(p, t, 0, partner).start()
 
         def forward(self, j):
@@ -324,7 +357,7 @@
         def finish(self):
             self.slot(p, t, 0, partner).wait_send()
             for j in around:
-                self.slot(p, t, j, in_plane(near[j])).wait_send()
+                self.slot(p, t, j, in_plane(spin[j])).wait_send()
                 self.slot(p, near[j], tensor + j, partner).wait_send()
 
     first = Gather(ag1, ag1_s, ag1_r)
@@ -336,6 +369,10 @@
             hidden_ref.at[:, lanes], hid.at[index], hid_s.at[j], hid_r.at[index], in_plane(near[j])
         )
 
+    for load in smalls:
+        load.wait()
+    for load in loads:
+        load.start()
     hidden = hidden_ref[...].astype(F32)
     ag1[p, t] = rms_scale(hidden, input_gain_ref[...]).astype(BF16)
 
@@ -436,29 +473,36 @@
     for index in range(devices):
         to_owner[index] = slots[index * deep : (index + 1) * deep]
 
-    def exchange(outgoing, incoming, sent, received):
-        def copy(j, index):
-            peer = lax.rem(me + j, devices)
-            slot = peer if index is None else index
-            return remote(
-                outgoing.at[peer], incoming.at[slot], sent.at[j], received.at[slot], place(peer)
-            )
-
-        for j in range(1, devices):
-            copy(j, me).start()
-        incoming[me] = outgoing[me]
-
-        def arrive():
-            for j in range(1, devices):
-                copy(j, None).wait_recv()
-
-        def finish():
-            for j in range(1, devices):
-                copy(j, me).wait_send()
-
-        return arrive, finish
-
-    arrive, sent_a1 = exchange(to_owner, at_owner, a1_s, a1_r)
+    own_group, own_seat = lax.div(me, per_kv), lax.rem(me, per_kv)
+    side_groups = kv_count // pool
+    depth = lax.rem(own_group, side_groups)
+    turns = [(0, 0)] + [(q, h) for q in (0, 1) for h in range(1, side_groups)] + [(1, 0)]
+    groups = [
+        (p if q == 0 else 1 - p) * side_groups + lax.rem(depth + h, side_groups) for q, h in turns
+    ]
+
+    def members(g):
+        if g == 0:
+            return [(j, groups[0] * per_kv + lax.rem(own_seat + j, per_kv)) for j in range(1, per_kv)]
+        return [(g * per_kv + j, groups[g] * per_kv + j) for j in range(per_kv)]
+
+    everyone = [member for g in range(kv_count) for member in members(g)]
+
+    def post(outgoing, incoming, sent, received, number, peer):
+        return remote(
+            outgoing.at[peer], incoming.at[me], sent.at[number], received.at[me], place(peer)
+        )
+
+    def arrival(outgoing, incoming, sent, received, number, peer):
+        return remote(
+            outgoing.at[peer], incoming.at[peer], sent.at[number], received.at[peer], place(peer)
+        )
+
+    one = (to_owner, at_owner, a1_s, a1_r)
+    two = (to_home, at_home, a2_s, a2_r)
+    for member in everyone[::-1]:
+        post(*one, *member).start()
+    at_owner[me] = to_owner[me]
 
     for j in around:
         hidden_copy(j, near[j]).wait_recv()
@@ -466,14 +510,16 @@
         hblock[index * rows : (index + 1) * rows, :] = hid[index].astype(F32)
     for load in loads[3:5]:
         load.wait()
-    arrive()
 
     scale_factor = 1.0 / math.sqrt(head_dim)
     copies = group * SLOTS // span
     allowed = jnp.tile(inside, (copies, 1)) > 0.5
     upper = iota((span, head_dim), 0) < SLOTS
     deep = heads_here * SLOTS
-    for k in range(kv_count):
+    for g in range(kv_count):
+        for member in members(g):
+            arrival(*one, *member).wait_recv()
+        k = groups[g]
         blocks = [at_owner[k * per_kv + j].astype(F32) for j in range(per_kv)]
         query = jnp.concatenate([b[:deep] for b in blocks], axis=0)
         both = blocks[0][deep:]
@@ -484,7 +530,7 @@
         own_value = jnp.tile(jnp.where(upper, turned_over, both), (copies, 1))
         own_key = jnp.tile(key_new.astype(BF16).astype(F32), (copies, 1))
         query = turn(query, query_gain_ref[...], copies).astype(BF16)
-        lanes = slice(k * head_dim, (k + 1) * head_dim)
+        lanes = pl.ds(pl.multiple_of(k * head_dim, head_dim), head_dim)
         scores = turned(query, kc[:, lanes]) * scale_factor
         own_score = jnp.sum(query.astype(F32) * own_key, axis=1, keepdims=True) * scale_factor
         scores = jnp.where(allowed, scores, -1e30)
@@ -497,10 +543,13 @@
         head_out = summed / denominator
         for j in range(per_kv):
             to_home[k * per_kv + j] = head_out[j * deep : (j + 1) * deep]
-
-    arrive, sent_a2 = exchange(to_home, at_home, a2_s, a2_r)
+        for member in members(g):
+            post(*two, *member).start()
+    at_home[me] = to_home[me]
+
     loads[5].wait()
-    arrive()
+    for member in everyone:
+        arrival(*two, *member).wait_recv()
     back = jnp.concatenate([at_home[index] for index in range(devices)], axis=0).astype(BF16)
     gathered = jnp.dot(gather_hot, back, preferred_element_type=F32).astype(BF16)
     head_rows = jnp.concatenate(
@@ -514,7 +563,8 @@
         return remote(part.at[c, 1 - p], peer.at[c], sent.at[c], received.at[c], partner)
 
     def products(left, weight, part, peer, sent, received, order):
-        for c in range(pairs):
+        wide = part.shape[-1]
+        for c in range(part.shape[0]):
             at = pl.ds(pl.multiple_of(order[c] * wide, wide), wide)
             product = jnp.dot(left, weight[:, at], preferred_element_type=F32)
             for q in range(pool):
@@ -573,19 +623,21 @@
     activated = (gate_part / (1.0 + jnp.exp(-gate_part)) * up_part).astype(BF16)
 
     loads[8].wait()
-    products(activated, dw, part2, peer2, sw2_s, sw2_r, list(range(pairs)))
+    cuts = part2.shape[0]
+    wide = width // cuts
+    products(activated, dw, part2, peer2, sw2_s, sw2_r, list(range(cuts)))
 
     def row_copy(c, j, slot):
         lanes = slice(c * wide, (c + 1) * wide)
         return remote(
-            out2.at[near[j], :, lanes],
+            out2.at[spin[j], :, lanes],
             in2.at[slot, :, lanes],
             rs2_s.at[c, j],
             rs2_r.at[c, slot],
-            in_plane(near[j]),
+            in_plane(spin[j]),
         )
 
-    for c in range(pairs):
+    for c in range(cuts):
         lanes = slice(c * wide, (c + 1) * wide)
         swap(part2, peer2, sw2_s, sw2_r, c).wait_recv()
         sum2[:, lanes] = peer2[c].astype(F32) + part2[c, p].astype(F32)
@@ -595,7 +647,7 @@
             row_copy(c, j, t).start()
 
     pick = hot(iota((8, requests), 1) == me * rows + iota((8, requests), 0))
-    mixed = jnp.concatenate(
+    mixed_ref[...] = jnp.concatenate(
         [
             jnp.dot(
                 pick,
@@ -606,30 +658,30 @@
         ],
         axis=1,
     )
-    mixed_ref[...] = mixed.astype(BF16)
     first.finish()
-    sent_a1()
-    sent_a2()
+    for member in everyone:
+        post(*one, *member).wait_send()
+        post(*two, *member).wait_send()
     second.finish()
     for j in around:
         hidden_copy(j, t).wait_send()
     for c in range(pairs):
         swap(part1, peer1, sw1_s, sw1_r, c).wait_send()
+    for c in range(cuts):
         swap(part2, peer2, sw2_s, sw2_r, c).wait_send()
     for c in range(pairs - 1):
         for i in range(2):
             block_copy(2 * c + i, 2 * turn_of[c] + i, t).wait_send()
     block_copy(tensor - 2, near[1], t).wait_send()
 
-    for c in range(pairs):
+    for c in range(cuts):
         lanes = slice(c * wide, (c + 1) * wide)
-        total = mixed[:, lanes]
-        lowered = out2[t, :, lanes].astype(F32)
+        total = out2[t, :, lanes].astype(F32)
         for j in around:
-            row_copy(c, j, near[j]).wait_recv()
-            lowered = lowered + in2[near[j], :, lanes].astype(F32)
-        final_ref[:, lanes] = (total + lowered).astype(BF16)
-    for c in range(pairs):
+            row_copy(c, j, spin[j]).wait_recv()
+            total = total + in2[spin[j], :, lanes].astype(F32)
+        added_ref[:, lanes] = total
+    for c in range(cuts):
         for j in around:
             row_copy(c, j, t).wait_send()
 
@@ -668,7 +720,17 @@
     gate_turned, up_turned = gate_weight.T, up_weight.T
     dma = pltpu.SemaphoreType.DMA
     deep = (heads_here + 2) * SLOTS
-    scratch = [
+    small = (
+        hidden,
+        request_slot[None, :],
+        lengths[None, :],
+        input_gain[None, :],
+        frequency,
+        query_gain[None, :],
+        key_gain[None, :],
+        post_gain[None, :],
+    )
+    scratch = [pltpu.VMEM(v.shape, v.dtype) for v in small] + [
         pltpu.VMEM(query_weight.shape, BF16),
         pltpu.VMEM((2 * key_cols, width), BF16),
         pltpu.VMEM(output_weight.shape, BF16),
@@ -690,11 +752,12 @@
         pltpu.VMEM((tensor, half, block), BF16),
         pltpu.VMEM((tensor, half, block), BF16),
         pltpu.VMEM((pool, tensor, half, block), BF16),
-        pltpu.VMEM((pairs, pool, half, 2 * block), BF16),
-        pltpu.VMEM((pairs, half, 2 * block), BF16),
+        pltpu.VMEM((CUTS, pool, half, width // CUTS), BF16),
+        pltpu.VMEM((CUTS, half, width // CUTS), BF16),
         pltpu.VMEM((half, width), F32),
         pltpu.VMEM((tensor, rows, width), BF16),
         pltpu.VMEM((tensor, rows, width), BF16),
+        dma((len(small),)),
         dma((9,)),
         dma((2 * tensor,)),
         dma((pool, tensor)),
@@ -710,32 +773,25 @@
         dma((pairs,)),
         dma((tensor,)),
         dma((tensor,)),
-        dma((pairs,)),
-        dma((pairs,)),
-        dma((pairs, tensor)),
-        dma((pairs, tensor)),
+        dma((CUTS,)),
+        dma((CUTS,)),
+        dma((CUTS, tensor)),
+        dma((CUTS, tensor)),
     ]
     vmem = pl.BlockSpec(memory_space=pltpu.VMEM)
     hbm = pl.BlockSpec(memory_space=pl.ANY)
-    row = jax.ShapeDtypeStruct(hidden.shape, BF16)
-    return pl.pallas_call(
+    row = pltpu.VMEM(hidden.shape, F32)
+    mixed, added = pl.pallas_call(
         functools.partial(step_kernel, pool, tensor),
         out_shape=(row, row),
-        in_specs=[vmem] * 8 + [hbm] * 9,
+        in_specs=[hbm] * (len(small) + 9),
         out_specs=(vmem, vmem),
         scratch_shapes=scratch,
         compiler_params=pltpu.CompilerParams(
             collective_id=0, has_side_effects=True, vmem_limit_bytes=62 * 1024 * 1024
         ),
     )(
-        hidden,
-        input_gain[None, :],
-        query_gain[None, :],
-        key_gain[None, :],
-        post_gain[None, :],
-        lengths[None, :],
-        request_slot[None, :],
-        frequency,
+        *small,
         query_weight,
         key_weight.T,
         value_weight.T,
@@ -746,6 +802,7 @@
         key_cache,
         value_cache,
     )
+    return mixed.astype(hidden.dtype), (mixed + added).astype(hidden.dtype)
 
 
 def dispatch(pool, tensor, *operands):

time: 56 us -> 51.2 us (0.914)
  local copies, waits for them, and re-layouts: 2.7 us -> 0 us
  Pallas kernels: 52.4 us -> 49.8 us
  other arithmetic: 0 us -> 0.64 us
    unnamed x2 -> x0, local copies, waits for them, and re-layouts: 2.7 us -> none
    pallas_call x1, Pallas kernels: 52.4 us -> 49.8 us  [fused(): pl.pallas_call(functools.partial(step_kernel, pool, tensor), out_shape=(r...]
    convert_element_type x0 -> x1, other arithmetic: none -> 0.64 us  [fused(): return (mixed.astype(hidden.dtype), (mixed + added).astype(hidden.dtype))]
where the time goes in v2:
time: 51.2 us; the launch traced here: 51 us
  Pallas kernels  49.8 us (97%)
  other arithmetic  0.64 us (1%)
  between operations  0.64 us (1%)
    pallas_call x1, Pallas kernels, fused(): pl.pallas_call(functools.partial(step_kernel, pool, tensor), out_shape=(r...  49.8 us

profile of v2, /device:TPU:0, one launch (start us, length us, event | category | flops | bytes accessed | tf_op | source)
XLA Modules:
  0.0 51.0 jit_solution(7085410433579673649)
XLA Ops:
  0.6 49.8 %shard_map.176 = (f32[2,5120]{1,0:T(2,128)S(1)}, f32[2,5120]{1,0:T(2,128)S(1)}) custom-call(bf16[2,5120]{1,0:T(2,128)(2,1)} %hidden_hbm.1, s32[1,32]{1,0:T(1,128)} %bitcast.16, s32[1,32]{1,0:T(1,128)} %bitcast.17, f32[1,5120]{1,0:T(1,128)} %bitcast.14, f32[1,128]{1,0:T(1,128)} %constant.2.clone.frequency_hbm, f32[1,128]{1,0:T(1,128)} %bitcast.18, ...), custom_call_target="tpu_custom_call" | custom-call | tf_op jit(solution)/shard_map/pallas_call | solution.py:784
  50.4 0.6 %add_convert_fusion = (bf16[2,5120]{1,0:T(2,128)(2,1)}, bf16[2,5120]{1,0:T(2,128)(2,1)}) fusion(f32[2,5120]{1,0:T(2,128)S(1)} %get-tuple-element.4, f32[2,5120]{1,0:T(2,128)S(1)} %get-tuple-element.5), kind=kLoop, calls=%fused_computation | loop fusion | flops 30720 | bytes 122880 | tf_op jit(solution)/shard_map/convert_element_type | solution.py:805

commit v3 on v2

--- a/solution.py
+++ b/solution.py
@@ -344,7 +344,7 @@
 
         def send(self):
             for j in around:
-                self.slot(p, t, j, in_plane(spin[j])).start()
+                self.slot(p, t, j, in_plane(near[j])).start()
             self.slot(p, t, 0, partner).start()
 
         def forward(self, j):
@@ -357,7 +357,7 @@
         def finish(self):
             self.slot(p, t, 0, partner).wait_send()
             for j in around:
-                self.slot(p, t, j, in_plane(spin[j])).wait_send()
+                self.slot(p, t, j, in_plane(near[j])).wait_send()
                 self.slot(p, near[j], tensor + j, partner).wait_send()
 
     first = Gather(ag1, ag1_s, ag1_r)
@@ -500,7 +500,7 @@
 
     one = (to_owner, at_owner, a1_s, a1_r)
     two = (to_home, at_home, a2_s, a2_r)
-    for member in everyone[::-1]:
+    for member in everyone:
         post(*one, *member).start()
     at_owner[me] = to_owner[me]
 
@@ -627,14 +627,9 @@
     wide = width // cuts
     products(activated, dw, part2, peer2, sw2_s, sw2_r, list(range(cuts)))
 
-    def row_copy(c, j, slot):
-        lanes = slice(c * wide, (c + 1) * wide)
+    def row_copy(j, slot):
         return remote(
-            out2.at[spin[j], :, lanes],
-            in2.at[slot, :, lanes],
-            rs2_s.at[c, j],
-            rs2_r.at[c, slot],
-            in_plane(spin[j]),
+            out2.at[spin[j]], in2.at[slot], rs2_s.at[j], rs2_r.at[slot], in_plane(spin[j])
         )
 
     for c in range(cuts):
@@ -643,8 +638,8 @@
         sum2[:, lanes] = peer2[c].astype(F32) + part2[c, p].astype(F32)
         for index in range(tensor):
             out2[index, :, lanes] = sum2[index * rows : (index + 1) * rows, lanes].astype(BF16)
-        for j in around:
-            row_copy(c, j, t).start()
+    for j in around:
+        row_copy(j, t).start()
 
     pick = hot(iota((8, requests), 1) == me * rows + iota((8, requests), 0))
     mixed_ref[...] = jnp.concatenate(
@@ -674,16 +669,13 @@
             block_copy(2 * c + i, 2 * turn_of[c] + i, t).wait_send()
     block_copy(tensor - 2, near[1], t).wait_send()
 
-    for c in range(cuts):
-        lanes = slice(c * wide, (c + 1) * wide)
-        total = out2[t, :, lanes].astype(F32)
-        for j in around:
-            row_copy(c, j, spin[j]).wait_recv()
-            total = total + in2[spin[j], :, lanes].astype(F32)
-        added_ref[:, lanes] = total
-    for c in range(cuts):
-        for j in around:
-            row_copy(c, j, t).wait_send()
+    total = out2[t].astype(F32)
+    for j in around:
+        row_copy(j, spin[j]).wait_recv()
+        total = total + in2[spin[j]].astype(F32)
+    added_ref[...] = total
+    for j in around:
+        row_copy(j, t).wait_send()
 
 
 def fused(pool, tensor, *operands):
@@ -775,8 +767,8 @@
         dma((tensor,)),
         dma((CUTS,)),
         dma((CUTS,)),
-        dma((CUTS, tensor)),
-        dma((CUTS, tensor)),
+        dma((tensor,)),
+        dma((tensor,)),
     ]
     vmem = pl.BlockSpec(memory_space=pltpu.VMEM)
     hbm = pl.BlockSpec(memory_space=pl.ANY)

time: 51.2 us -> 49.7 us (0.971)
  Pallas kernels: 49.8 us -> 48.2 us
    pallas_call x1, Pallas kernels: 49.8 us -> 48.2 us  [fused(): pl.pallas_call(functools.partial(step_kernel, pool, tensor), out_shape=(r...]
where the time goes in v3:
time: 49.7 us; the launch traced here: 49.5 us
  Pallas kernels  48.2 us (97%)
  other arithmetic  0.64 us (1%)
  between operations  0.64 us (1%)
    pallas_call x1, Pallas kernels, fused(): pl.pallas_call(functools.partial(step_kernel, pool, tensor), out_shape=(r...  48.2 us

profile of v3, /device:TPU:0, one launch (start us, length us, event | category | flops | bytes accessed | tf_op | source)
XLA Modules:
  0.0 49.5 jit_solution(13610704418888044642)
XLA Ops:
  0.6 48.2 %shard_map.176 = (f32[2,5120]{1,0:T(2,128)S(1)}, f32[2,5120]{1,0:T(2,128)S(1)}) custom-call(bf16[2,5120]{1,0:T(2,128)(2,1)} %hidden_hbm.1, s32[1,32]{1,0:T(1,128)} %bitcast.16, s32[1,32]{1,0:T(1,128)} %bitcast.17, f32[1,5120]{1,0:T(1,128)} %bitcast.14, f32[1,128]{1,0:T(1,128)} %constant.2.clone.frequency_hbm, f32[1,128]{1,0:T(1,128)} %bitcast.18, ...), custom_call_target="tpu_custom_call" | custom-call | tf_op jit(solution)/shard_map/pallas_call | solution.py:776
  48.8 0.6 %add_convert_fusion = (bf16[2,5120]{1,0:T(2,128)(2,1)}, bf16[2,5120]{1,0:T(2,128)(2,1)}) fusion(f32[2,5120]{1,0:T(2,128)S(1)} %get-tuple-element.4, f32[2,5120]{1,0:T(2,128)S(1)} %get-tuple-element.5), kind=kLoop, calls=%fused_computation | loop fusion | flops 30720 | bytes 122880 | tf_op jit(solution)/shard_map/convert_element_type | solution.py:797

commit v4 on v3

--- a/solution.py
+++ b/solution.py
@@ -335,17 +335,17 @@
         return {"pool": p, "tensor": other}
 
     class Gather:
-        def __init__(self, buffer, sent, received):
-            self.buffer, self.sent, self.received = buffer, sent, received
+        def __init__(self, buffer, sent, received, order):
+            self.buffer, self.sent, self.received, self.order = buffer, sent, received, order
 
         def slot(self, q, index, k, where):
             at = self.buffer.at[q, index]
             return remote(at, at, self.sent.at[k], self.received.at[q, index], where)
 
         def send(self):
+            self.slot(p, t, 0, partner).start()
             for j in around:
-                self.slot(p, t, j, in_plane(near[j])).start()
-            self.slot(p, t, 0, partner).start()
+                self.slot(p, t, j, in_plane(self.order[j])).start()
 
         def forward(self, j):
             self.slot(p, near[j], tensor + j, partner).wait_recv()
@@ -357,11 +357,11 @@
         def finish(self):
             self.slot(p, t, 0, partner).wait_send()
             for j in around:
-                self.slot(p, t, j, in_plane(near[j])).wait_send()
+                self.slot(p, t, j, in_plane(self.order[j])).wait_send()
                 self.slot(p, near[j], tensor + j, partner).wait_send()
 
-    first = Gather(ag1, ag1_s, ag1_r)
-    second = Gather(mb, ag2_s, ag2_r)
+    first = Gather(ag1, ag1_s, ag1_r, spin)
+    second = Gather(mb, ag2_s, ag2_r, near)
 
     def hidden_copy(j, index):
         lanes = pl.ds(pl.multiple_of(near[j] * block, block), block)
@@ -440,13 +440,13 @@
 
     pl.semaphore_wait(barrier, devices - 1)
     first.send()
-    for j in around:
-        hidden_copy(j, t).start()
     hid[t] = hidden_ref[:, pl.ds(pl.multiple_of(t * block, block), block)]
     for load in loads[:3]:
         load.wait()
     for j in around:
         first.forward(j)
+    for j in around:
+        hidden_copy(j, t).start()
     for index in range(tensor):
         xs[p, index * rows : (index + 1) * rows, :] = ag1[p, index].astype(F32)
     for j in range(tensor):
@@ -484,7 +484,10 @@
     def members(g):
         if g == 0:
             return [(j, groups[0] * per_kv + lax.rem(own_seat + j, per_kv)) for j in range(1, per_kv)]
-        return [(g * per_kv + j, groups[g] * per_kv + j) for j in range(per_kv)]
+        return [
+            (g * per_kv + j, groups[g] * per_kv + lax.rem(own_seat + j, per_kv))
+            for j in range(per_kv)
+        ]
 
     everyone = [member for g in range(kv_count) for member in members(g)]
 

time: 49.7 us -> 49.3 us (level)
  no operation moved by 1% of the time
where the time goes in v4:
time: 49.3 us; the launch traced here: 49.1 us
  Pallas kernels  47.8 us (97%)
  other arithmetic  0.64 us (1%)
  between operations  0.64 us (1%)
    pallas_call x1, Pallas kernels, fused(): pl.pallas_call(functools.partial(step_kernel, pool, tensor), out_shape=(r...  47.8 us

profile of v4, /device:TPU:0, one launch (start us, length us, event | category | flops | bytes accessed | tf_op | source)
XLA Modules:
  0.0 49.1 jit_solution(997734262161104128)
XLA Ops:
  0.6 47.8 %shard_map.176 = (f32[2,5120]{1,0:T(2,128)S(1)}, f32[2,5120]{1,0:T(2,128)S(1)}) custom-call(bf16[2,5120]{1,0:T(2,128)(2,1)} %hidden_hbm.1, s32[1,32]{1,0:T(1,128)} %bitcast.16, s32[1,32]{1,0:T(1,128)} %bitcast.17, f32[1,5120]{1,0:T(1,128)} %bitcast.14, f32[1,128]{1,0:T(1,128)} %constant.2.clone.frequency_hbm, f32[1,128]{1,0:T(1,128)} %bitcast.18, ...), custom_call_target="tpu_custom_call" | custom-call | tf_op jit(solution)/shard_map/pallas_call | solution.py:779
  48.4 0.6 %add_convert_fusion = (bf16[2,5120]{1,0:T(2,128)(2,1)}, bf16[2,5120]{1,0:T(2,128)(2,1)}) fusion(f32[2,5120]{1,0:T(2,128)S(1)} %get-tuple-element.4, f32[2,5120]{1,0:T(2,128)S(1)} %get-tuple-element.5), kind=kLoop, calls=%fused_computation | loop fusion | flops 30720 | bytes 122880 | tf_op jit(solution)/shard_map/convert_element_type | solution.py:800

commit v5 on v4

--- a/solution.py
+++ b/solution.py
@@ -438,6 +438,11 @@
     def turned(left, weight):
         return lax.dot_general(left, weight, (((1,), (1,)), ((), ())), preferred_element_type=F32)
 
+    wide = iota((2 * key_cols, 2 * head_dim), 1)
+    tall = iota((2 * key_cols, 2 * head_dim), 0)
+    shift = lax.rem(me, per_kv) * key_cols
+    aim = jnp.where(tall < key_cols, tall + shift, tall - key_cols + head_dim + shift)
+    shift_hot = hot(aim == wide)
     pl.semaphore_wait(barrier, devices - 1)
     first.send()
     hid[t] = hidden_ref[:, pl.ds(pl.multiple_of(t * block, block), block)]
@@ -448,21 +453,17 @@
     for j in around:
         hidden_copy(j, t).start()
     for index in range(tensor):
-        xs[p, index * rows : (index + 1) * rows, :] = ag1[p, index].astype(F32)
+        xs[p, index * rows : (index + 1) * rows, :] = ag1[p, index]
     for j in range(tensor):
         first.across(j)
     for index in range(tensor):
-        xs[1 - p, index * rows : (index + 1) * rows, :] = ag1[1 - p, index].astype(F32)
-
-    left = jnp.concatenate([xs[q] for q in range(pool)], axis=0).astype(BF16)
+        xs[1 - p, index * rows : (index + 1) * rows, :] = ag1[1 - p, index]
+
+    left = jnp.concatenate([xs[q] for q in range(pool)], axis=0)
     query_part = jnp.dot(left, qw[...], preferred_element_type=F32).astype(BF16)
     kv_part = turned(left, kvw[...]).astype(BF16)
 
-    wide = iota((2 * key_cols, 2 * head_dim), 1)
-    tall = iota((2 * key_cols, 2 * head_dim), 0)
-    shift = lax.rem(me, per_kv) * key_cols
-    aim = jnp.where(tall < key_cols, tall + shift, tall - key_cols + head_dim + shift)
-    kv_wide = jnp.dot(kv_part, hot(aim == wide), preferred_element_type=F32).astype(BF16)
+    kv_wide = jnp.dot(kv_part, shift_hot, preferred_element_type=F32).astype(BF16)
     stacked = jnp.concatenate(
         [query_part[:, i * head_dim : (i + 1) * head_dim] for i in range(heads_here)]
         + [kv_wide[:, :head_dim], kv_wide[:, head_dim:]],
@@ -737,7 +738,7 @@
         pltpu.VMEM((pool, tensor, rows, width), BF16),
         pltpu.VMEM((tensor, rows, block), BF16),
         pltpu.VMEM((half, block), F32),
-        pltpu.VMEM((pool, half, width), F32),
+        pltpu.VMEM((pool, half, width), BF16),
         pltpu.VMEM((devices, deep, head_dim), BF16),
         pltpu.VMEM((devices, deep, head_dim), BF16),
         pltpu.VMEM((devices, heads_here * SLOTS, head_dim), F32),

time: 49.3 us -> 49.2 us (level)
  no operation moved by 1% of the time
where the time goes in v5:
time: 49.2 us; the launch traced here: 49 us
  Pallas kernels  47.7 us (97%)
  other arithmetic  0.64 us (1%)
  between operations  0.64 us (1%)
    pallas_call x1, Pallas kernels, fused(): pl.pallas_call(functools.partial(step_kernel, pool, tensor), out_shape=(r...  47.7 us

profile of v5, /device:TPU:0, one launch (start us, length us, event | category | flops | bytes accessed | tf_op | source)
XLA Modules:
  0.0 49.0 jit_solution(8533593754166876463)
XLA Ops:
  0.6 47.7 %shard_map.176 = (f32[2,5120]{1,0:T(2,128)S(1)}, f32[2,5120]{1,0:T(2,128)S(1)}) custom-call(bf16[2,5120]{1,0:T(2,128)(2,1)} %hidden_hbm.1, s32[1,32]{1,0:T(1,128)} %bitcast.16, s32[1,32]{1,0:T(1,128)} %bitcast.17, f32[1,5120]{1,0:T(1,128)} %bitcast.14, f32[1,128]{1,0:T(1,128)} %constant.2.clone.frequency_hbm, f32[1,128]{1,0:T(1,128)} %bitcast.18, ...), custom_call_target="tpu_custom_call" | custom-call | tf_op jit(solution)/shard_map/pallas_call | solution.py:780
  48.3 0.6 %add_convert_fusion = (bf16[2,5120]{1,0:T(2,128)(2,1)}, bf16[2,5120]{1,0:T(2,128)(2,1)}) fusion(f32[2,5120]{1,0:T(2,128)S(1)} %get-tuple-element.4, f32[2,5120]{1,0:T(2,128)S(1)} %get-tuple-element.5), kind=kLoop, calls=%fused_computation | loop fusion | flops 30720 | bytes 122880 | tf_op jit(solution)/shard_map/convert_element_type | solution.py:801
